TPU v7x, 512 devices: a whole 4x4x16 slice. The times are simulated.
512 devices in a mesh: gx: 32 (over y, x, core), vert: 16 (over z).
Axes of the slice: x: 4, y: 4, z: 16, core: 2. Of those that a mesh axis runs over, the one named last changes fastest.
Arguments:
- state: float32 [256, 16, 16384], P('gx', None, 'vert'), may hold values from -6 to 6
- macro: float32 [5, 256, 16], P(None, 'gx'), may hold values from -4 to 4
- relax_rate: float32 [256, 16], P('gx'), may hold values from 0.01 to 300, as said below
- velocity: float32 [3, 16384], P(None, 'vert'), may hold values from -2 to 4
- vel_sign: int32 [16384], P('vert'), may hold values from 0 to 1, as said below
- quad_weight: float32 [16384], P('vert'), may hold values from 0.5 to 2
- freestream: float32 [16, 16384], P(None, 'vert'), may hold values from -6 to 6
- wall_flag: int32 [16], replicated, may hold values 0 or 1
Outputs:
- new_state: float32 [256, 16, 16384], P('gx', None, 'vert')
- new_macro: float32 [5, 256, 16], P(None, 'gx')
Inputs may be any that keep to these rules, and one draw needn't show every extreme that they name: Each row of relax_rate varies from cell to cell. `vel_sign`: every aligned block of 1024 velocities holds both signs.
All inputs are finite; a program needn't handle non-finite values.
Results may differ from a plain program's by a relative error of at most 0.00013.
Values sent between devices are 32-bit elements; how exact they have to be, the bound alone decides.
No kernel may reach another device: no remote copies, remote signals or barrier semaphores. Data moves between devices by JAX's collectives and lax.ppermute only.
A program may use at most 64 MiB of HBM per device.

v0:
```python
import jax
import jax.numpy as jnp
from jax import lax
from jax.sharding import PartitionSpec as P

exact_mode = lax.Precision.HIGHEST


def prefix(value, axis, join, neutral, backward):
    count, mine = (lax.axis_size(axis), lax.axis_index(axis))
    pieces = jax.tree.map(lambda part: lax.all_gather(part, axis), value)
    if backward:
        pieces = jax.tree.map(lambda part: part[::-1], pieces)
        mine = count - 1 - mine
    total = jax.tree.map(
        lambda part, zero: jnp.full_like(part, 0) + jnp.asarray(zero, part.dtype), value, neutral
    )

    def turn(position, total):
        longer = join(total, jax.tree.map(lambda part: part[position], pieces))
        return jax.tree.map(lambda new, old: jnp.where(position < mine, new, old), longer, total)

    return lax.fori_loop(0, count - 1, turn, total)


def with_halo(cells, sides, width):
    for axis, dim in sides:
        count = lax.axis_size(axis)
        ends = count - 1
        head = lax.slice_in_dim(cells, 0, width, axis=dim)
        tail = lax.slice_in_dim(cells, cells.shape[dim] - width, cells.shape[dim], axis=dim)
        cells = jnp.concatenate(
            [
                lax.ppermute(tail, axis, [(i, (i + 1) % count) for i in range(ends)]),
                cells,
                lax.ppermute(head, axis, [((i + 1) % count, i) for i in range(ends)]),
            ],
            axis=dim,
        )
    return cells


def basis_sets(velocity, vel_sign, quad_weight, groups):
    magnitude = velocity[0]
    along_x = jnp.where(vel_sign == 1, magnitude, -magnitude)
    along_y = velocity[1]
    along_z = velocity[2]
    square = along_x * along_x + along_y * along_y + along_z * along_z
    ones_row = jnp.ones_like(along_x)
    equil_basis = jnp.stack([ones_row, 2.0 * along_x, 2.0 * along_y, 2.0 * along_z, square - 1.5])
    weights = quad_weight / (quad_weight.shape[0] * groups)
    heat_factor = 0.2 * (square - 2.5)
    moment_rows = jnp.stack(
        [
            ones_row,
            along_x,
            along_y,
            along_z,
            2.0 / 3.0 * square - 1.0,
            2.0 * along_x * along_y,
            2.0 * along_x * along_z,
            2.0 * along_y * along_z,
            2.0 * (along_x * along_x - square / 3.0),
            2.0 * (along_y * along_y - square / 3.0),
            heat_factor * along_x,
            heat_factor * along_y,
            heat_factor * along_z,
        ]
    )
    outflux = jnp.where(vel_sign == 0, weights * magnitude, 0.0)
    influx = jnp.where(vel_sign == 1, weights * magnitude, 0.0)
    return (magnitude, equil_basis, moment_rows * weights, outflux, influx)


def compose(earlier, latter):
    return (latter[0] * earlier[0], latter[0] * earlier[1] + latter[1])


def march_zero(decay, driven, reverse):

    def advance_cell(carried, pieces):
        zero_run = pieces[0] * carried[0] + pieces[1]
        product = pieces[0] * carried[1]
        return ((zero_run, product), (zero_run, product))

    initial = (jnp.zeros_like(driven[0]), jnp.ones_like(driven[0]))
    _, (zero_runs, products) = lax.scan(advance_cell, initial, (decay, driven), reverse=reverse)
    return (zero_runs, products)


def advance(padded, relax_cells):
    conserved = padded[:5]
    flow_x = jnp.stack(
        [
            padded[1],
            padded[0] + padded[4] + padded[8],
            padded[5],
            padded[6],
            2.0 / 3.0 * (padded[1] + padded[10]),
        ]
    )
    flow_y = jnp.stack(
        [
            padded[2],
            padded[5],
            padded[0] + padded[4] + padded[9],
            padded[7],
            2.0 / 3.0 * (padded[2] + padded[11]),
        ]
    )
    centre = conserved[:, 1:-1, 1:-1]
    laplace = (
        conserved[:, 2:, 1:-1]
        + conserved[:, :-2, 1:-1]
        + conserved[:, 1:-1, 2:]
        + conserved[:, 1:-1, :-2]
        - 4.0 * centre
    )
    divergence = (
        flow_x[:, 2:, 1:-1] - flow_x[:, :-2, 1:-1] + flow_y[:, 1:-1, 2:] - flow_y[:, 1:-1, :-2]
    )
    diffusivity = 0.2 / (1.0 + relax_cells)
    return (centre + diffusivity * laplace - 0.25 * divergence, centre)


def local(state, macro, relax_rate, velocity, vel_sign, quad_weight, freestream, wall_flag):
    cells_x = state.shape[0]
    cells_y = state.shape[1]
    vel_count = state.shape[2]
    slab_count = lax.axis_size("gx")
    slab_index = lax.axis_index("gx")
    magnitude, equil_basis, moment_basis, outflux, influx = basis_sets(
        velocity, vel_sign, quad_weight, lax.axis_size("vert")
    )
    courant = cells_x * slab_count * magnitude
    relax_cell = relax_rate[:, :, None]
    flat_macro = macro.reshape(macro.shape[0], cells_x * cells_y)
    equil_state = jnp.einsum("kc,kv->cv", flat_macro, equil_basis, precision=exact_mode).reshape(
        cells_x, cells_y, vel_count
    )
    source = state + relax_cell * equil_state
    wall_mask = wall_flag[:, None] == 1
    wall_in = jnp.sum(influx) / slab_count
    divisor = 1.0 + courant + relax_cell
    decay = courant / divisor
    driven = source / divisor
    back_runs, back_products = march_zero(decay, driven, True)
    fore_runs, fore_products = march_zero(decay, driven, False)
    ones_plane = jnp.ones((cells_y, vel_count), jnp.float32)
    zero_plane = jnp.zeros((cells_y, vel_count), jnp.float32)
    back_maps = prefix(
        (back_products[0], back_runs[0]), "gx", compose, (ones_plane, zero_plane), True
    )
    entry_back = back_maps[0] * freestream + back_maps[1]
    back = back_products * entry_back + back_runs
    at_anchor = slab_index == 0
    wall_out = jnp.where(at_anchor, jnp.dot(back[0], outflux, precision=exact_mode), 0.0)
    wall_out, wall_in = lax.psum((wall_out, wall_in), ("gx", "vert"))
    rho_wall = wall_out / wall_in
    inflow_left = jnp.where(wall_mask, rho_wall[:, None], freestream)
    fore_maps = prefix(
        (fore_products[-1], fore_runs[-1]), "gx", compose, (ones_plane, zero_plane), False
    )
    entry_fore = fore_maps[0] * inflow_left + fore_maps[1]
    fore = fore_products * entry_fore + fore_runs
    kinetic = jnp.where(vel_sign == 1, fore, back)
    flattened = kinetic.reshape(cells_x * cells_y, vel_count)
    partial_value = jnp.einsum("cv,kv->kc", flattened, moment_basis, precision=exact_mode).reshape(
        13, cells_x, cells_y
    )
    moments = lax.psum(partial_value, "vert")
    padded = with_halo(moments, (("gx", 1),), 1)
    padded = jnp.concatenate([padded[:, :, -1:], padded, padded[:, :, :1]], axis=2)
    updated, centre = advance(padded, relax_rate)
    change = updated - centre
    flat_change = change.reshape(change.shape[0], cells_x * cells_y)
    correction = jnp.einsum("kc,kv->cv", flat_change, equil_basis, precision=exact_mode).reshape(
        cells_x, cells_y, vel_count
    )
    return (kinetic + correction, updated)


def solution(mesh):
    return jax.shard_map(
        local,
        mesh=mesh,
        in_specs=(
            P("gx", None, "vert"),
            P(None, "gx", None),
            P("gx", None),
            P(None, "vert"),
            P("vert"),
            P("vert"),
            P(None, "vert"),
            P(),
        ),
        out_specs=(P("gx", None, "vert"), P(None, "gx", None)),
        check_vma=False,
    )
```

profile of v0, /device:TPU:7, one launch (start us, length us, event | category | flops | bytes accessed | tf_op | source)
XLA Modules:
  0.0 472.6 jit_solution(17301780224435400815)
XLA Ops:
  9.6 1.9 select_reduce_fusion
  12.1 1.2 add_divide_fusion
  19.7 58.5 %all-gather.9.cloned.1.call-done = f32[32,16,1024]{2,1,0:T(8,128)} async-done(((f32[1,16,1024]{2,1,0:T(8,128)}), f32[32,16,1024]{2,1,0:T(8,128)}) %all-gather.9.cloned.1.call-update) | async-done | bytes 2097168 | tf_op jit(solution)/shard_map/all_gather | solution.py:11
  78.2 1.7 rev.6
  79.9 59.8 %all-gather.11.cloned.1.call-done = f32[32,16,1024]{2,1,0:T(8,128)} async-done(((f32[1,16,1024]{2,1,0:T(8,128)}), f32[32,16,1024]{2,1,0:T(8,128)}) %all-gather.11.cloned.1.call-update) | async-done | bytes 2097168 | tf_op jit(solution)/shard_map/all_gather | solution.py:11
  139.6 3.2 rev.7
  142.9 28.3 %while.71 = (s32[]{:T(128)}, f32[16,1024]{1,0:T(8,128)S(1)}, f32[16,1024]{1,0:T(8,128)S(1)}, s32[]{:T(128)}, f32[32,16,1024]{2,1,0:T(8,128)S(1)}, /*index=5*/f32[32,16,1024]{2,1,0:T(8,128)}, s32[]{:T(128)}, s32[]{:T(128)}) while((s32[]{:T(128)}, f32[16,1024]{1,0:T(8,128)S(1)}, f32[16,1024]{1,0:T(8,128)S(1)}, s32[]{:T(128)}, ...), condition=%wide.region_7.8_spmd.clone, body=%wide.region_6.7_spmd.clone.sunk | while | flops 114692 | bytes 393325 | solution.py:23
  172.4 28.8 %all-gather.5.cloned.1.call-done = f32[32,16,1024]{2,1,0:T(8,128)} async-done(((f32[1,16,1024]{2,1,0:T(8,128)}), f32[32,16,1024]{2,1,0:T(8,128)}) %all-gather.5.cloned.1.call-update) | async-done | bytes 2097168 | tf_op jit(solution)/shard_map/all_gather | solution.py:11
  201.2 61.3 %all-gather.7.cloned.1.call-done = f32[32,16,1024]{2,1,0:T(8,128)} async-done(((f32[1,16,1024]{2,1,0:T(8,128)}), f32[32,16,1024]{2,1,0:T(8,128)}) %all-gather.7.cloned.1.call-update) | async-done | bytes 2097168 | tf_op jit(solution)/shard_map/all_gather | solution.py:11
  262.6 29.2 %while.70 = (s32[]{:T(128)}, f32[16,1024]{1,0:T(8,128)S(1)}, f32[16,1024]{1,0:T(8,128)S(1)}, s32[]{:T(128)}, f32[32,16,1024]{2,1,0:T(8,128)}, /*index=5*/f32[32,16,1024]{2,1,0:T(8,128)}, s32[]{:T(128)}, s32[]{:T(128)}) while((s32[]{:T(128)}, f32[16,1024]{1,0:T(8,128)S(1)}, f32[16,1024]{1,0:T(8,128)S(1)}, s32[]{:T(128)}, ...), condition=%wide.region_3.4_spmd.clone, body=%wide.region_2.3_spmd.clone.sunk | while | flops 114692 | bytes 393325 | solution.py:23
  262.6 0.9 fusion.39
  263.5 0.9 fusion.39
  264.4 0.9 fusion.39
  265.4 0.9 fusion.39
  266.3 0.9 fusion.39
  267.3 0.9 fusion.39
  268.2 0.9 fusion.39
  269.2 0.9 fusion.39
  270.1 0.9 fusion.39
  271.1 0.9 fusion.39
  272.0 0.9 fusion.39
  272.9 0.9 fusion.39
  273.9 0.9 fusion.39
  274.8 0.9 fusion.39
  275.8 0.9 fusion.39
  276.7 0.9 fusion.39
  277.7 0.9 fusion.39
  278.6 0.9 fusion.39
  279.6 0.9 fusion.39
  280.5 0.9 fusion.39
  281.4 0.9 fusion.39
  282.4 0.9 fusion.39
  283.3 0.9 fusion.39
  284.3 0.9 fusion.39
  285.2 0.9 fusion.39
  286.2 0.9 fusion.39
  287.1 0.9 fusion.39
  288.0 0.9 fusion.39
  289.0 0.9 fusion.39
  289.9 0.9 fusion.39
  290.9 0.9 fusion.39
  291.8 103.7 %all-reduce = (f32[16]{0:T(128)S(1)}, f32[]{:T(128)}) all-reduce(f32[16]{0:T(128)S(1)} %fusion.2, f32[]{:T(128)S(6)} %div.41), channel_id=1, replica_groups=mesh['gx'=32,'vert'=16] {'gx','vert'}, use_global_device_ids=true, to_apply=%region_8.9 | all-reduce | flops 17 | bytes 136 | tf_op jit(solution)/shard_map/psum | solution.py:158
  396.4 1.9 fusion.3
  398.4 40.2 %psum.23 = f32[13,8,16]{2,0,1:T(8,128)S(1)} all-reduce(f32[13,8,16]{2,0,1:T(8,128)S(1)} %fusion.3), channel_id=1, replica_groups=mesh['gx'=32,'vert'=16] {'vert'}, use_global_device_ids=true, to_apply=%region_11.12 | all-reduce | flops 1664 | bytes 13312 | tf_op jit(solution)/shard_map/psum | solution.py:171
  438.6 17.3 %collective-permute-start.1 = (f32[13,1,16]{2,0,1:T(8,128)S(1)}, f32[13,1,16]{2,0,1:T(8,128)S(1)}, u32[]{:S(2)}, u32[]{:S(2)}) collective-permute-start(f32[13,1,16]{2,0,1:T(8,128)S(1)} %get-tuple-element.544), channel_id=1, source_target_pairs={{0,16},{16,32},{32,48},{48,64},{64,80},{80,96},{96,112},{112,128},... | collective-permute-start | bytes 2504 | tf_op jit(solution)/shard_map/ppermute | solution.py:34
  455.9 1.9 collective-permute-start
  457.9 5.1 %collective-permute-done = f32[13,1,16]{2,0,1:T(8,128)S(1)} collective-permute-done((f32[13,1,16]{2,0,1:T(8,128)S(1)}, f32[13,1,16]{2,0,1:T(8,128)S(1)}, u32[]{:S(2)}, u32[]{:S(2)}) %collective-permute-start) | collective-permute-done | bytes 864 | tf_op jit(solution)/shard_map/ppermute | solution.py:36
  464.0 1.5 convolution_add_fusion
  (127 shorter events, 40.4 us)
Async XLA Ops:
  7.2 71.0 %all-gather.9.cloned.1.call-start = ((), (), s32[]{:S(2)}) async-start(), calls=%async_computation.2 | async-start | bytes 2162688 | tf_op jit(solution)/shard_map/all_gather | solution.py:11
  9.6 4.0 copy-start.7
  14.7 125.0 %all-gather.11.cloned.1.call-start = ((), (), s32[]{:S(2)}) async-start(), calls=%async_computation.3 | async-start | bytes 2162688 | tf_op jit(solution)/shard_map/all_gather | solution.py:11
  15.4 185.8 %all-gather.5.cloned.1.call-start = ((), (), s32[]{:S(2)}) async-start(), calls=%async_computation | async-start | bytes 2162688 | tf_op jit(solution)/shard_map/all_gather | solution.py:11
  15.5 2.1 copy-start.5
  15.5 2.2 copy-start.10
  16.2 3.5 copy-start
  16.2 3.5 copy-start.2
  16.9 245.7 %all-gather.7.cloned.1.call-start = ((), (), s32[]{:S(2)}) async-start(), calls=%async_computation.1 | async-start | bytes 2162688 | tf_op jit(solution)/shard_map/all_gather | solution.py:11
  171.2 225.0 %copy-start.4 = (f32[16,1024]{1,0:T(8,128)S(1)}, f32[16,1024]{1,0:T(8,128)}, u32[]{:S(2)}) copy-start(f32[16,1024]{1,0:T(8,128)} %param.22) | copy-start | bytes 196612
  171.2 225.0 %copy-start.9 = (pred[16]{0:T(512)(128)(4,1)S(1)}, pred[16]{0:T(512)(128)(4,1)}, u32[]{:S(2)}) copy-start(pred[16]{0:T(512)(128)(4,1)} %broadcast_compare_fusion.1) | copy-start | bytes 52
  172.1 224.2 %copy-start.1 = (f32[8,16,1024]{2,1,0:T(8,128)S(1)}, f32[8,16,1024]{2,1,0:T(8,128)}, u32[]{:S(2)}) copy-start(f32[8,16,1024]{2,1,0:T(8,128)} %copy-done) | copy-start | bytes 1572868
  172.1 224.2 %copy-start.3 = (f32[8,16,1024]{2,1,0:T(8,128)S(1)}, f32[8,16,1024]{2,1,0:T(8,128)}, u32[]{:S(2)}) copy-start(f32[8,16,1024]{2,1,0:T(8,128)} %copy-done.2) | copy-start | bytes 1572868
  172.1 224.2 %copy-start.8 = (pred[1024]{0:T(1024)(128)(4,1)S(1)}, pred[1024]{0:T(1024)(128)(4,1)}, u32[]{:S(2)}) copy-start(pred[1024]{0:T(1024)(128)(4,1)} %copy-done.7) | copy-start | bytes 3076
  291.8 164.1 %copy-start.6 = (f32[8,16]{1,0:T(8,128)S(1)}, f32[8,16]{1,0:T(8,128)}, u32[]{:S(2)}) copy-start(f32[8,16]{1,0:T(8,128)} %param.18) | copy-start | bytes 1540
  438.6 19.3 %collective-permute-start.1 = (f32[13,1,16]{2,0,1:T(8,128)S(1)}, f32[13,1,16]{2,0,1:T(8,128)S(1)}, u32[]{:S(2)}, u32[]{:S(2)}) collective-permute-start(f32[13,1,16]{2,0,1:T(8,128)S(1)} %get-tuple-element.544), channel_id=1, source_target_pairs={{0,16},{16,32},{32,48},{48,64},{64,80},{80,96},{96,112},{112,128},... | collective-permute-start | bytes 2504 | tf_op jit(solution)/shard_map/ppermute | solution.py:34
  455.9 7.1 %collective-permute-start = (f32[13,1,16]{2,0,1:T(8,128)S(1)}, f32[13,1,16]{2,0,1:T(8,128)S(1)}, u32[]{:S(2)}, u32[]{:S(2)}) collective-permute-start(f32[13,1,16]{2,0,1:T(8,128)S(1)} %get-tuple-element.543), channel_id=1, source_target_pairs={{16,0},{32,16},{48,32},{64,48},{80,64},{96,80},{112,96},{128,112},... | collective-permute-start | bytes 2504 | tf_op jit(solution)/shard_map/ppermute | solution.py:36
Sparse Core Ops, SparseCore 0:
  14.8 63.3 all-gather.8
  81.3 58.3 all-gather.10
  142.8 58.3 all-gather.4
  204.2 58.3 all-gather.6
where the time goes:
time: 476 us; the launch traced here: 473 us
  waiting for transfers between devices  214 us (45%)
  blocking collectives  144 us (30%)
  other arithmetic  64.6 us (14%)
  starting transfers between devices  19.4 us (4%)
  between operations  14.8 us (3%)
  local copies, waits for them, and re-layouts  10.4 us (2%)
    all_gather x4, waiting for transfers between devices, prefix(): pieces = jax.tree.map(lambda part: lax.all_gather(part, axis), value)  208 us
    psum x1, blocking collectives, local(): wall_out, wall_in = lax.psum((wall_out, wall_in), ('gx', 'vert'))  104 us
    select_n x62, other arithmetic, turn(): jnp.where(position < mine, new, old)  56.1 us
    psum x1, blocking collectives, local(): moments = lax.psum(partial_value, 'vert')  40.2 us
    ppermute x1, starting transfers between devices, with_halo(): lax.ppermute(tail, axis, [(i, (i + 1) % count) for i in range(ends)])  17.3 us
  transfers between devices with their start and end apart: 6, of which 5 were waited for; matrix products, arithmetic and copies ran while one was open for 8% of the time, Pallas kernels for 0%

commit v1 on v0

--- a/solution.py
+++ b/solution.py
@@ -168,7 +168,9 @@
     partial_value = jnp.einsum("cv,kv->kc", flattened, moment_basis, precision=exact_mode).reshape(
         13, cells_x, cells_y
     )
-    moments = lax.psum(partial_value, "vert")
+    moments = partial_value
+    for hop in (1, 2, 4, 8):
+        moments = moments + lax.ppermute(moments, "vert", [(dev, dev ^ hop) for dev in range(16)])
     padded = with_halo(moments, (("gx", 1),), 1)
     padded = jnp.concatenate([padded[:, :, -1:], padded, padded[:, :, :1]], axis=2)
     updated, centre = advance(padded, relax_rate)

time: 476 us -> 461 us (0.968)
  blocking collectives: 144 us -> 104 us
  waiting for transfers between devices: 214 us -> 228 us
  starting transfers between devices: 19.4 us -> 27 us
    psum x1 -> x0, blocking collectives: 40.2 us -> none  [local(): moments = lax.psum(partial_value, 'vert')]
    ppermute x0 -> x4, waiting for transfers between devices: none -> 18.6 us  [local(): lax.ppermute(moments, 'vert', [(dev, dev ^ hop) for dev in range(16)])]
    ppermute x0 -> x4, starting transfers between devices: none -> 16.8 us  [local(): lax.ppermute(moments, 'vert', [(dev, dev ^ hop) for dev in range(16)])]
    ppermute x1, starting transfers between devices: 17.3 us -> 3 us  [with_halo(): lax.ppermute(tail, axis, [(i, (i + 1) % count) for i in range(ends)])]
    ppermute x1, starting transfers between devices: 1.92 us -> 7.05 us  [with_halo(): lax.ppermute(head, axis, [((i + 1) % count, i) for i in range(ends)])]
    ppermute x1, waiting for transfers between devices: 5.12 us -> 0.01 us  [with_halo(): lax.ppermute(head, axis, [((i + 1) % count, i) for i in range(ends)])]
  transfers between devices with their start and end apart: 6 -> 10, of which waited for: 5 -> 9; matrix products, arithmetic and copies ran while one was open for 8% -> 8% of each run, Pallas kernels for 0% -> 0%
where the time goes in v1:
time: 461 us; the launch traced here: 454 us
  waiting for transfers between devices  228 us (49%)
  blocking collectives  104 us (23%)
  other arithmetic  64.7 us (14%)
  starting transfers between devices  27 us (6%)
  between operations  14.9 us (3%)
  local copies, waits for them, and re-layouts  10.4 us (2%)
    all_gather x4, waiting for transfers between devices, prefix(): pieces = jax.tree.map(lambda part: lax.all_gather(part, axis), value)  208 us
    psum x1, blocking collectives, local(): wall_out, wall_in = lax.psum((wall_out, wall_in), ('gx', 'vert'))  104 us
    select_n x62, other arithmetic, turn(): jnp.where(position < mine, new, old)  56.1 us
    ppermute x4, waiting for transfers between devices, local(): lax.ppermute(moments, 'vert', [(dev, dev ^ hop) for dev in range(16)])  18.6 us
    ppermute x4, starting transfers between devices, local(): lax.ppermute(moments, 'vert', [(dev, dev ^ hop) for dev in range(16)])  16.8 us
  transfers between devices with their start and end apart: 10, of which 9 were waited for; matrix products, arithmetic and copies ran while one was open for 8% of the time, Pallas kernels for 0%

profile of v1, /device:TPU:7, one launch (start us, length us, event | category | flops | bytes accessed | tf_op | source)
XLA Modules:
  0.0 454.5 jit_solution(2442360994557481985)
XLA Ops:
  9.6 1.9 select_reduce_fusion
  12.2 1.2 add_divide_fusion
  19.6 58.5 %all-gather.9.cloned.1.call-done = f32[32,16,1024]{2,1,0:T(8,128)} async-done(((f32[1,16,1024]{2,1,0:T(8,128)}), f32[32,16,1024]{2,1,0:T(8,128)}) %all-gather.9.cloned.1.call-update) | async-done | bytes 2097168 | tf_op jit(solution)/shard_map/all_gather | solution.py:11
  78.2 1.7 rev.6
  79.9 59.8 %all-gather.11.cloned.1.call-done = f32[32,16,1024]{2,1,0:T(8,128)} async-done(((f32[1,16,1024]{2,1,0:T(8,128)}), f32[32,16,1024]{2,1,0:T(8,128)}) %all-gather.11.cloned.1.call-update) | async-done | bytes 2097168 | tf_op jit(solution)/shard_map/all_gather | solution.py:11
  139.7 3.2 rev.7
  142.9 28.3 %while.71 = (s32[]{:T(128)}, f32[16,1024]{1,0:T(8,128)S(1)}, f32[16,1024]{1,0:T(8,128)S(1)}, s32[]{:T(128)}, f32[32,16,1024]{2,1,0:T(8,128)S(1)}, /*index=5*/f32[32,16,1024]{2,1,0:T(8,128)}, s32[]{:T(128)}, s32[]{:T(128)}) while((s32[]{:T(128)}, f32[16,1024]{1,0:T(8,128)S(1)}, f32[16,1024]{1,0:T(8,128)S(1)}, s32[]{:T(128)}, ...), condition=%wide.region_7.8_spmd.clone, body=%wide.region_6.7_spmd.clone.sunk | while | flops 114692 | bytes 393325 | solution.py:23
  172.4 28.8 %all-gather.5.cloned.1.call-done = f32[32,16,1024]{2,1,0:T(8,128)} async-done(((f32[1,16,1024]{2,1,0:T(8,128)}), f32[32,16,1024]{2,1,0:T(8,128)}) %all-gather.5.cloned.1.call-update) | async-done | bytes 2097168 | tf_op jit(solution)/shard_map/all_gather | solution.py:11
  201.2 61.3 %all-gather.7.cloned.1.call-done = f32[32,16,1024]{2,1,0:T(8,128)} async-done(((f32[1,16,1024]{2,1,0:T(8,128)}), f32[32,16,1024]{2,1,0:T(8,128)}) %all-gather.7.cloned.1.call-update) | async-done | bytes 2097168 | tf_op jit(solution)/shard_map/all_gather | solution.py:11
  262.5 29.2 %while.70 = (s32[]{:T(128)}, f32[16,1024]{1,0:T(8,128)S(1)}, f32[16,1024]{1,0:T(8,128)S(1)}, s32[]{:T(128)}, f32[32,16,1024]{2,1,0:T(8,128)}, /*index=5*/f32[32,16,1024]{2,1,0:T(8,128)}, s32[]{:T(128)}, s32[]{:T(128)}) while((s32[]{:T(128)}, f32[16,1024]{1,0:T(8,128)S(1)}, f32[16,1024]{1,0:T(8,128)S(1)}, s32[]{:T(128)}, ...), condition=%wide.region_3.4_spmd.clone, body=%wide.region_2.3_spmd.clone.sunk | while | flops 114692 | bytes 393325 | solution.py:23
  263.4 0.9 fusion.39
  264.4 0.9 fusion.39
  265.3 0.9 fusion.39
  266.3 0.9 fusion.39
  267.2 0.9 fusion.39
  268.2 0.9 fusion.39
  269.1 0.9 fusion.39
  270.0 0.9 fusion.39
  271.0 0.9 fusion.39
  271.9 0.9 fusion.39
  272.9 0.9 fusion.39
  273.8 0.9 fusion.39
  274.8 0.9 fusion.39
  275.7 0.9 fusion.39
  276.7 0.9 fusion.39
  277.6 0.9 fusion.39
  278.5 0.9 fusion.39
  279.5 0.9 fusion.39
  280.4 0.9 fusion.39
  281.4 0.9 fusion.39
  282.3 0.9 fusion.39
  283.3 0.9 fusion.39
  285.2 0.9 fusion.39
  287.0 0.9 fusion.39
  288.9 0.9 fusion.39
  291.8 103.7 %all-reduce = (f32[16]{0:T(128)S(1)}, f32[]{:T(128)}) all-reduce(f32[16]{0:T(128)S(1)} %fusion.2, f32[]{:T(128)S(6)} %div.41), channel_id=1, replica_groups=mesh['gx'=32,'vert'=16] {'gx','vert'}, use_global_device_ids=true, to_apply=%region_8.9 | all-reduce | flops 17 | bytes 136 | tf_op jit(solution)/shard_map/psum | solution.py:158
  396.4 1.9 fusion.3
  398.3 1.9 collective-permute-start
  400.2 3.1 collective-permute-done
  403.3 2.3 collective-permute-start.1
  405.6 4.1 collective-permute-done.1
  409.7 4.0 collective-permute-start.2
  413.7 6.4 %collective-permute-done.2 = f32[13,8,16]{2,0,1:T(8,128)S(1)} collective-permute-done((f32[13,8,16]{2,0,1:T(8,128)S(1)}, f32[13,8,16]{2,0,1:T(8,128)S(1)}, u32[]{:S(2)}, u32[]{:S(2)}) %collective-permute-start.2) | collective-permute-done | bytes 6688 | tf_op jit(solution)/shard_map/ppermute | solution.py:173
  420.1 8.6 %collective-permute-start.3 = (f32[13,8,16]{2,0,1:T(8,128)S(1)}, f32[13,8,16]{2,0,1:T(8,128)S(1)}, u32[]{:S(2)}, u32[]{:S(2)}) collective-permute-start(f32[13,8,16]{2,0,1:T(8,128)S(1)} %add.208), channel_id=1, source_target_pairs={{0,8},{1,9},{2,10},{3,11},{4,12},{5,13},{6,14},{7,15},{8,0},{9,1},... | collective-permute-start | bytes 19976 | tf_op jit(solution)/shard_map/ppermute | solution.py:173
  428.7 5.1 %collective-permute-done.3 = f32[13,8,16]{2,0,1:T(8,128)S(1)} collective-permute-done((f32[13,8,16]{2,0,1:T(8,128)S(1)}, f32[13,8,16]{2,0,1:T(8,128)S(1)}, u32[]{:S(2)}, u32[]{:S(2)}) %collective-permute-start.3) | collective-permute-done | bytes 6688 | tf_op jit(solution)/shard_map/ppermute | solution.py:173
  433.8 7.1 %collective-permute-start.4 = (f32[13,1,16]{2,0,1:T(8,128)S(1)}, f32[13,1,16]{2,0,1:T(8,128)S(1)}, u32[]{:S(2)}, u32[]{:S(2)}) collective-permute-start(f32[13,1,16]{2,0,1:T(8,128)S(1)} %get-tuple-element.543), channel_id=1, source_target_pairs={{16,0},{32,16},{48,32},{64,48},{80,64},{96,80},{112,96},{128,112},... | collective-permute-start | bytes 2504 | tf_op jit(solution)/shard_map/ppermute | solution.py:36
  440.9 3.0 collective-permute-start.5
  445.9 1.5 convolution_add_fusion
  (138 shorter events, 46.7 us)
Async XLA Ops:
  7.2 71.0 %all-gather.9.cloned.1.call-start = ((), (), s32[]{:S(2)}) async-start(), calls=%async_computation.2 | async-start | bytes 2162688 | tf_op jit(solution)/shard_map/all_gather | solution.py:11
  9.6 4.0 copy-start.7
  14.7 125.0 %all-gather.11.cloned.1.call-start = ((), (), s32[]{:S(2)}) async-start(), calls=%async_computation.3 | async-start | bytes 2162688 | tf_op jit(solution)/shard_map/all_gather | solution.py:11
  15.4 185.7 %all-gather.5.cloned.1.call-start = ((), (), s32[]{:S(2)}) async-start(), calls=%async_computation | async-start | bytes 2162688 | tf_op jit(solution)/shard_map/all_gather | solution.py:11
  15.5 2.2 copy-start.5
  15.5 2.2 copy-start.10
  16.2 3.5 copy-start
  16.2 3.5 copy-start.2
  16.9 245.6 %all-gather.7.cloned.1.call-start = ((), (), s32[]{:S(2)}) async-start(), calls=%async_computation.1 | async-start | bytes 2162688 | tf_op jit(solution)/shard_map/all_gather | solution.py:11
  171.2 224.9 %copy-start.4 = (f32[16,1024]{1,0:T(8,128)S(1)}, f32[16,1024]{1,0:T(8,128)}, u32[]{:S(2)}) copy-start(f32[16,1024]{1,0:T(8,128)} %param.22) | copy-start | bytes 196612
  171.2 224.9 %copy-start.9 = (pred[16]{0:T(512)(128)(4,1)S(1)}, pred[16]{0:T(512)(128)(4,1)}, u32[]{:S(2)}) copy-start(pred[16]{0:T(512)(128)(4,1)} %broadcast_compare_fusion.1) | copy-start | bytes 52
  172.1 224.1 %copy-start.1 = (f32[8,16,1024]{2,1,0:T(8,128)S(1)}, f32[8,16,1024]{2,1,0:T(8,128)}, u32[]{:S(2)}) copy-start(f32[8,16,1024]{2,1,0:T(8,128)} %copy-done) | copy-start | bytes 1572868
  172.1 224.1 %copy-start.3 = (f32[8,16,1024]{2,1,0:T(8,128)S(1)}, f32[8,16,1024]{2,1,0:T(8,128)}, u32[]{:S(2)}) copy-start(f32[8,16,1024]{2,1,0:T(8,128)} %copy-done.2) | copy-start | bytes 1572868
  172.2 224.1 %copy-start.8 = (pred[1024]{0:T(1024)(128)(4,1)S(1)}, pred[1024]{0:T(1024)(128)(4,1)}, u32[]{:S(2)}) copy-start(pred[1024]{0:T(1024)(128)(4,1)} %copy-done.7) | copy-start | bytes 3076
  291.8 152.1 %copy-start.6 = (f32[8,16]{1,0:T(8,128)S(1)}, f32[8,16]{1,0:T(8,128)}, u32[]{:S(2)}) copy-start(f32[8,16]{1,0:T(8,128)} %param.18) | copy-start | bytes 1540
  398.3 5.0 %collective-permute-start = (f32[13,8,16]{2,0,1:T(8,128)S(1)}, f32[13,8,16]{2,0,1:T(8,128)S(1)}, u32[]{:S(2)}, u32[]{:S(2)}) collective-permute-start(f32[13,8,16]{2,0,1:T(8,128)S(1)} %fusion.3), channel_id=1, source_target_pairs={{0,1},{1,0},{2,3},{3,2},{4,5},{5,4},{6,7},{7,6},{8,9},{9,8},{10,11... | collective-permute-start | bytes 19976 | tf_op jit(solution)/shard_map/ppermute | solution.py:173
  403.3 6.3 %collective-permute-start.1 = (f32[13,8,16]{2,0,1:T(8,128)S(1)}, f32[13,8,16]{2,0,1:T(8,128)S(1)}, u32[]{:S(2)}, u32[]{:S(2)}) collective-permute-start(f32[13,8,16]{2,0,1:T(8,128)S(1)} %add.206), channel_id=1, source_target_pairs={{0,2},{1,3},{2,0},{3,1},{4,6},{5,7},{6,4},{7,5},{8,10},{9,11},{10,... | collective-permute-start | bytes 19976 | tf_op jit(solution)/shard_map/ppermute | solution.py:173
  409.7 10.4 %collective-permute-start.2 = (f32[13,8,16]{2,0,1:T(8,128)S(1)}, f32[13,8,16]{2,0,1:T(8,128)S(1)}, u32[]{:S(2)}, u32[]{:S(2)}) collective-permute-start(f32[13,8,16]{2,0,1:T(8,128)S(1)} %add.207), channel_id=1, source_target_pairs={{0,4},{1,5},{2,6},{3,7},{4,0},{5,1},{6,2},{7,3},{8,12},{9,13},{10,... | collective-permute-start | bytes 19976 | tf_op jit(solution)/shard_map/ppermute | solution.py:173
  420.1 13.7 %collective-permute-start.3 = (f32[13,8,16]{2,0,1:T(8,128)S(1)}, f32[13,8,16]{2,0,1:T(8,128)S(1)}, u32[]{:S(2)}, u32[]{:S(2)}) collective-permute-start(f32[13,8,16]{2,0,1:T(8,128)S(1)} %add.208), channel_id=1, source_target_pairs={{0,8},{1,9},{2,10},{3,11},{4,12},{5,13},{6,14},{7,15},{8,0},{9,1},... | collective-permute-start | bytes 19976 | tf_op jit(solution)/shard_map/ppermute | solution.py:173
  433.8 10.1 %collective-permute-start.4 = (f32[13,1,16]{2,0,1:T(8,128)S(1)}, f32[13,1,16]{2,0,1:T(8,128)S(1)}, u32[]{:S(2)}, u32[]{:S(2)}) collective-permute-start(f32[13,1,16]{2,0,1:T(8,128)S(1)} %get-tuple-element.543), channel_id=1, source_target_pairs={{16,0},{32,16},{48,32},{64,48},{80,64},{96,80},{112,96},{128,112},... | collective-permute-start | bytes 2504 | tf_op jit(solution)/shard_map/ppermute | solution.py:36
  440.9 3.8 collective-permute-start.5
Sparse Core Ops, SparseCore 0:
  14.8 63.3 all-gather.8
  81.3 58.3 all-gather.10
  142.8 58.3 all-gather.4
  204.1 58.3 all-gather.6
